TPU v7x, 512 devices: a whole 4x4x16 slice. The times are simulated.
512 devices in a mesh: blk: 256 (over z, y, x_lo, core), dp: 2 (over x_hi).
Axes of the slice: x: 4 (x_hi: 2, x_lo: 2; x = x_hi * 2 + x_lo), y: 4, z: 16, core: 2. Of those that a mesh axis runs over, the one named last changes fastest.
Arguments:
- acts: bfloat16 [2, 73728, 2048], P(None, ('blk', 'dp')), may hold values from -6 to 6
- cotangent: bfloat16 [2, 73728, 2048], P(None, ('blk', 'dp')), may hold values from -6 to 6
- w_gate: bfloat16 [256, 2048, 128], P('blk', 'dp'), may hold values from -0.125 to 0.125
- w_up: bfloat16 [256, 2048, 128], P('blk', 'dp'), may hold values from -0.125 to 0.125
- w_down: bfloat16 [256, 128, 2048], P('blk', None, 'dp'), may hold values from -0.078125 to 0.078125
- slab_layer: int32 [256], replicated, may hold values from 0 to 1
Outputs:
- grad_gate: bfloat16 [256, 2048, 128], P('blk', 'dp')
- grad_up: bfloat16 [256, 2048, 128], P('blk', 'dp')
- grad_down: bfloat16 [256, 128, 2048], P('blk', None, 'dp')
- acts_grad: bfloat16 [2, 73728, 2048], P(None, ('blk', 'dp'))
All inputs are finite; a program needn't handle non-finite values.
Results may differ from a plain program's by a relative error of at most 0.0049.
Values may be sent and summed in bfloat16 or wider, within the bound.
No kernel may reach another device: no remote copies, remote signals or barrier semaphores. Data moves between devices by JAX's collectives and lax.ppermute only.
A program may use at most 64 MiB of HBM per device.

v0:
```python
import jax
import jax.numpy as jnp
from jax import lax
from jax.sharding import PartitionSpec as P

TICKS = 3


def laid_out(parts, dim):
    shape = list(parts.shape[1:])
    shape[dim] *= parts.shape[0]
    return jnp.moveaxis(parts, 0, dim).reshape(shape)


def from_everyone(array, axis):
    peers = lax.axis_size(axis)
    return lax.all_to_all(
        jnp.broadcast_to(array[None], (peers, *array.shape)), axis, 0, 0, tiled=True
    )


def gather_directly(array, axis, dim):
    return laid_out(from_everyone(array, axis), dim)


def side_by_side(arrays, axis, dim, along):
    ends, at = ([], 0)
    for a in arrays[:-1]:
        at += a.shape[along]
        ends.append(at)
    both = jnp.concatenate(arrays, axis=along)
    return tuple(jnp.split(gather_directly(both, axis, dim), ends, axis=along))


def shifted(block, axis, distance):
    devices = range(lax.axis_size(axis))
    route = [((i - distance) % len(devices), i) for i in devices]
    return lax.ppermute(block, axis, route)


def in_blocks(array, dim, peers):
    before, after = (array.shape[:dim], array.shape[dim + 1 :])
    return jnp.moveaxis(array.reshape(*before, peers, -1, *after), dim, 0)


def sent_and_summed(array, axis, dim):
    peers = lax.axis_size(axis)
    parts = lax.all_to_all(in_blocks(array, dim, peers), axis, 0, 0, tiled=True)
    return jnp.sum(parts, axis=0)


def sent_together(arrays, axis, dim, along):
    both = jnp.concatenate(arrays, axis=along)
    filled, at, outs = (sent_and_summed(both, axis, dim), 0, [])
    for a in arrays:
        outs.append(lax.slice_in_dim(filled, at, at + a.shape[along], axis=along))
        at += a.shape[along]
    return tuple(outs)


def slab_terms(rows_x, rows_g, w_gate, w_up, w_down):
    gate = jnp.dot(rows_x, w_gate, preferred_element_type=jnp.float32)
    upward = jnp.dot(rows_x, w_up, preferred_element_type=jnp.float32)
    sigmoid_gate = jax.nn.sigmoid(gate)
    activated = gate * sigmoid_gate
    hidden = (activated * upward).astype(jnp.bfloat16)
    by_units = (((1,), (1,)), ((), ()))
    by_rows = (((0,), (0,)), ((), ()))
    hidden_grad = lax.dot_general(rows_g, w_down, by_units, preferred_element_type=jnp.float32)
    up_in = (hidden_grad * activated).astype(jnp.bfloat16)
    gate_in = (hidden_grad * upward * sigmoid_gate * (1.0 + gate * (1.0 - sigmoid_gate))).astype(
        jnp.bfloat16
    )
    grad_gate = lax.dot_general(rows_x, gate_in, by_rows, preferred_element_type=jnp.float32)
    grad_upw = lax.dot_general(rows_x, up_in, by_rows, preferred_element_type=jnp.float32)
    grad_down = lax.dot_general(hidden, rows_g, by_rows, preferred_element_type=jnp.float32)
    input_grad = lax.dot_general(gate_in, w_gate, by_units, preferred_element_type=jnp.float32)
    input_grad = input_grad + lax.dot_general(
        up_in, w_up, by_units, preferred_element_type=jnp.float32
    )
    return ((grad_gate, grad_upw, grad_down), input_grad)


def layer_rows(stack, layer):
    return lax.dynamic_index_in_dim(stack, layer, 0, keepdims=False)


def add_layer(total, layer, piece):
    current = lax.dynamic_index_in_dim(total, layer, 0, keepdims=False)
    return lax.dynamic_update_index_in_dim(total, current + piece, layer, 0)


def add_terms(first, second):
    return (first[0] + second[0], first[1] + second[1], first[2] + second[2])


def on_device(acts, cotangent, w_gate, w_up, w_down, slab_layer):
    whole = (*side_by_side((w_gate, w_up), "dp", 1, 0), gather_directly(w_down, "dp", 2))
    own_slab = (whole[0][0], whole[1][0], whole[2][0])
    cycle_size = lax.axis_size("blk")
    position = lax.axis_index("blk")
    input_total = jnp.zeros(acts.shape, jnp.float32)
    sums = None
    for tick in range(TICKS):
        layer = slab_layer[(position - tick) % cycle_size]
        if tick == 0:
            rows_x = layer_rows(acts, layer)
            rows_g = layer_rows(cotangent, layer)
        else:
            rows_x, rows_g = shifted(
                (layer_rows(acts, layer), layer_rows(cotangent, layer)), "blk", -tick
            )
        terms, input_grad = slab_terms(rows_x, rows_g, own_slab[0], own_slab[1], own_slab[2])
        sums = terms if tick == 0 else add_terms(sums, terms)
        if tick == 0:
            input_total = add_layer(input_total, layer, input_grad)
        else:
            returned = shifted(input_grad, "blk", tick)
            input_total = add_layer(input_total, layer, returned)
    halves = (*sent_together((sums[0], sums[1]), "dp", 0, 1), sent_and_summed(sums[2], "dp", 1))
    return (
        halves[0].astype(jnp.bfloat16)[None],
        halves[1].astype(jnp.bfloat16)[None],
        halves[2].astype(jnp.bfloat16)[None],
        input_total.astype(jnp.bfloat16),
    )


def solution(mesh):
    in_specs = (
        P(None, ("blk", "dp"), None),
        P(None, ("blk", "dp"), None),
        P("blk", "dp", None),
        P("blk", "dp", None),
        P("blk", None, "dp"),
        P(),
    )
    out_specs = (
        P("blk", "dp", None),
        P("blk", "dp", None),
        P("blk", None, "dp"),
        P(None, ("blk", "dp"), None),
    )
    return jax.shard_map(
        on_device, mesh=mesh, in_specs=in_specs, out_specs=out_specs, check_vma=False
    )
```

profile of v0, /device:TPU:283, one launch (start us, length us, event | category | flops | bytes accessed | tf_op | source)
XLA Modules:
  0.0 172.7 jit_solution(3487241331162543283)
XLA Ops:
  2.7 3.5 %all-to-all-start = ((bf16[2,1,128,1024]{2,3,1,0:T(8,128)(2,1)}), bf16[2,1,128,1024]{2,3,1,0:T(8,128)(2,1)S(1)}, u32[]{:S(2)}, u32[]{:S(2)}) async-start(bf16[2,1,128,1024]{2,3,1,0:T(8,128)(2,1)} %broadcast_in_dim.35), calls=%async_computation | async-start | bytes 1048576 | tf_op jit(solution)/shard_map/all_to_all | solution.py:17
  10.8 4.3 %all-to-all-done = bf16[2,1,128,1024]{2,3,1,0:T(8,128)(2,1)S(1)} async-done(((bf16[2,1,128,1024]{2,3,1,0:T(8,128)(2,1)}), bf16[2,1,128,1024]{2,3,1,0:T(8,128)(2,1)S(1)}, u32[]{:S(2)}, u32[]{:S(2)}) %all-to-all-start) | async-done | bytes 524320 | tf_op jit(solution)/shard_map/all_to_all | solution.py:17
  16.2 3.7 %all-to-all-start.1 = ((bf16[2,2,1024,128]{3,2,1,0:T(8,128)(2,1)}), bf16[2,2,1024,128]{3,2,1,0:T(8,128)(2,1)S(1)}, u32[]{:S(2)}, u32[]{:S(2)}) async-start(bf16[2,2,1024,128]{3,2,1,0:T(8,128)(2,1)} %broadcast_in_dim.36), calls=%async_computation.1 | async-start | bytes 2097152 | tf_op jit(solution)/shard_map/all_to_all | solution.py:17
  21.1 3.4 %collective-permute-start = (bf16[144,2048]{1,0:T(8,128)(2,1)}, bf16[144,2048]{1,0:T(8,128)(2,1)S(1)}, u32[]{:S(2)}, u32[]{:S(2)}) collective-permute-start(bf16[144,2048]{1,0:T(8,128)(2,1)} %get-tuple-element.11), channel_id=1, source_target_pairs={{2,0},{4,2},{6,4},{8,6},{10,8},{12,10},{14,12},{16,14},{18,16},{20... | collective-permute-start | bytes 1769480 | tf_op jit(solution)/shard_map/ppermute | solution.py:38
  25.6 1.9 %collective-permute-start.1 = (bf16[144,2048]{1,0:T(8,128)(2,1)}, bf16[144,2048]{1,0:T(8,128)(2,1)}, u32[]{:S(2)}, u32[]{:S(2)}) collective-permute-start(bf16[144,2048]{1,0:T(8,128)(2,1)} %get-tuple-element.9), channel_id=1, source_target_pairs={{2,0},{4,2},{6,4},{8,6},{10,8},{12,10},{14,12},{16,14},{18,16},{20... | collective-permute-start | bytes 1769480 | tf_op jit(solution)/shard_map/ppermute | solution.py:38
  27.6 2.7 %collective-permute-start.2 = (bf16[144,2048]{1,0:T(8,128)(2,1)}, bf16[144,2048]{1,0:T(8,128)(2,1)S(1)}, u32[]{:S(2)}, u32[]{:S(2)}) collective-permute-start(bf16[144,2048]{1,0:T(8,128)(2,1)} %get-tuple-element.10), channel_id=1, source_target_pairs={{4,0},{6,2},{8,4},{10,6},{12,8},{14,10},{16,12},{18,14},{20,16},{2... | collective-permute-start | bytes 1769480 | tf_op jit(solution)/shard_map/ppermute | solution.py:38
  30.3 2.8 %collective-permute-start.3 = (bf16[144,2048]{1,0:T(8,128)(2,1)}, bf16[144,2048]{1,0:T(8,128)(2,1)}, u32[]{:S(2)}, u32[]{:S(2)}) collective-permute-start(bf16[144,2048]{1,0:T(8,128)(2,1)} %get-tuple-element.8), channel_id=1, source_target_pairs={{4,0},{6,2},{8,4},{10,6},{12,8},{14,10},{16,12},{18,14},{20,16},{2... | collective-permute-start | bytes 1769480 | tf_op jit(solution)/shard_map/ppermute | solution.py:38
  35.0 1.5 fusion.4
  43.1 4.7 %collective-permute-done.2 = bf16[144,2048]{1,0:T(8,128)(2,1)S(1)} collective-permute-done((bf16[144,2048]{1,0:T(8,128)(2,1)}, bf16[144,2048]{1,0:T(8,128)(2,1)S(1)}, u32[]{:S(2)}, u32[]{:S(2)}) %collective-permute-start.2) | collective-permute-done | bytes 589856 | tf_op jit(solution)/shard_map/ppermute | solution.py:38
  48.8 1.4 multiply_convert_fusion.7
  50.6 10.1 %collective-permute-done.3 = bf16[144,2048]{1,0:T(8,128)(2,1)} collective-permute-done((bf16[144,2048]{1,0:T(8,128)(2,1)}, bf16[144,2048]{1,0:T(8,128)(2,1)}, u32[]{:S(2)}, u32[]{:S(2)}) %collective-permute-start.3) | collective-permute-done | bytes 589856 | tf_op jit(solution)/shard_map/ppermute | solution.py:38
  60.7 1.4 multiply_convert_fusion.6
  63.3 1.5 copy.23
  64.8 1.4 convolution_add_fusion.4
  66.2 1.4 convolution_add_fusion.3
  68.8 4.5 %all-to-all-start.3 = ((f32[2,128,1024]{2,1,0:T(8,128)}), f32[2,128,1024]{2,1,0:T(8,128)S(1)}, u32[]{:S(2)}, u32[]{:S(2)}) async-start(f32[2,128,1024]{2,1,0:T(8,128)} %bitcast.108), calls=%async_computation.3 | async-start | bytes 2097152 | tf_op jit(solution)/shard_map/all_to_all | solution.py:48
  73.5 1.4 convolution_add_fusion.1
  74.9 24.1 %collective-permute-start.4 = (f32[144,2048]{1,0:T(8,128)}, f32[144,2048]{1,0:T(8,128)}, u32[]{:S(2)}, u32[]{:S(2)}) collective-permute-start(f32[144,2048]{1,0:T(8,128)} %convolution_add_fusion.1), channel_id=1, source_target_pairs={{510,0},{0,2},{2,4},{4,6},{6,8},{8,10},{10,12},{12,14},{14,16},{16... | collective-permute-start | bytes 3538952 | tf_op jit(solution)/shard_map/ppermute | solution.py:38
  100.0 4.8 %all-to-all-start.2 = ((f32[2,1024,256]{1,2,0:T(8,128)}), f32[2,1024,256]{1,2,0:T(8,128)}, u32[]{:S(2)}, u32[]{:S(2)}) async-start(f32[2,1024,256]{1,2,0:T(8,128)} %bitcast.106), calls=%async_computation.2 | async-start | bytes 4194304 | tf_op jit(solution)/shard_map/all_to_all | solution.py:48
  108.1 8.5 %collective-permute-start.5 = (f32[144,2048]{1,0:T(8,128)}, f32[144,2048]{1,0:T(8,128)}, u32[]{:S(2)}, u32[]{:S(2)}) collective-permute-start(f32[144,2048]{1,0:T(8,128)} %convolution_add_fusion), channel_id=1, source_target_pairs={{508,0},{510,2},{0,4},{2,6},{4,8},{6,10},{8,12},{10,14},{12,16},{1... | collective-permute-start | bytes 3538952 | tf_op jit(solution)/shard_map/ppermute | solution.py:38
  118.5 46.1 %all-to-all-done.2 = f32[2,1024,256]{1,2,0:T(8,128)} async-done(((f32[2,1024,256]{1,2,0:T(8,128)}), f32[2,1024,256]{1,2,0:T(8,128)}, u32[]{:S(2)}, u32[]{:S(2)}) %all-to-all-start.2) | async-done | bytes 2097184 | tf_op jit(solution)/shard_map/all_to_all | solution.py:48
  164.6 1.8 %reduce_sum.18 = bf16[1024,256]{0,1:T(8,128)(2,1)S(1)} reduce(f32[2,1024,256]{1,2,0:T(8,128)} %all-to-all-done.2, f32[]{:T(128)} %constant.69.clone.1), dimensions={0}, to_apply=%region_0.1 | reduce | flops 262144 | bytes 2621444 | tf_op jit(solution)/shard_map/reduce_sum | solution.py:49
  168.2 1.8 %bitcast_dynamic-update-slice_fusion.1 = f32[2,144,2048]{2,1,0:T(8,128)S(1)} fusion(f32[2,144,2048]{2,1,0:T(8,128)S(1)} %fusion.1, s32[]{:T(128)S(6)} %select_n.50, f32[144,2048]{1,0:T(8,128)} %collective-permute-done.4, f32[1,144,2048]{2,1,0:T(8,128)} %constant_dynamic-slice_fusion.1), kind=kLoop, calls=%fused_computation.15 | loop fusion | flops 294912 | bytes 3538948 | tf_op jit(solution)/shard_map/jit(dynamic_update_index_in_dim)/dynamic_update_slice | solution.py:90
  170.1 1.5 bitcast_dynamic-update-slice_fusion
  (66 shorter events, 25.7 us)
Async XLA Ops:
  0.6 5.6 %copy-start.11 = (s32[256]{0:T(256)S(1)}, s32[256]{0:T(256)}, u32[]{:S(2)}) copy-start(s32[256]{0:T(256)} %param.11) | copy-start | bytes 3076
  0.6 10.1 %copy-start.9 = (bf16[1,1024,128]{2,1,0:T(8,128)(2,1)S(1)}, bf16[1,1024,128]{2,1,0:T(8,128)(2,1)}, u32[]{:S(2)}) copy-start(bf16[1,1024,128]{2,1,0:T(8,128)(2,1)} %param.9) | copy-start | bytes 786436
  0.7 10.1 %copy-start.10 = (bf16[1,1024,128]{2,1,0:T(8,128)(2,1)S(1)}, bf16[1,1024,128]{2,1,0:T(8,128)(2,1)}, u32[]{:S(2)}) copy-start(bf16[1,1024,128]{2,1,0:T(8,128)(2,1)} %param.8) | copy-start | bytes 786436
  2.7 12.4 %all-to-all-start = ((bf16[2,1,128,1024]{2,3,1,0:T(8,128)(2,1)}), bf16[2,1,128,1024]{2,3,1,0:T(8,128)(2,1)S(1)}, u32[]{:S(2)}, u32[]{:S(2)}) async-start(bf16[2,1,128,1024]{2,3,1,0:T(8,128)(2,1)} %broadcast_in_dim.35), calls=%async_computation | async-start | bytes 1048576 | tf_op jit(solution)/shard_map/all_to_all | solution.py:17
  15.1 1.1 copy-start.7
  16.2 3.7 %copy-start = (bf16[2,144,2048]{2,1,0:T(8,128)(2,1)S(1)}, bf16[2,144,2048]{2,1,0:T(8,128)(2,1)}, u32[]{:S(2)}) copy-start(bf16[2,144,2048]{2,1,0:T(8,128)(2,1)} %param.6) | copy-start | bytes 3538948
  16.2 20.3 %all-to-all-start.1 = ((bf16[2,2,1024,128]{3,2,1,0:T(8,128)(2,1)}), bf16[2,2,1024,128]{3,2,1,0:T(8,128)(2,1)S(1)}, u32[]{:S(2)}, u32[]{:S(2)}) async-start(bf16[2,2,1024,128]{3,2,1,0:T(8,128)(2,1)} %broadcast_in_dim.36), calls=%async_computation.1 | async-start | bytes 2097152 | tf_op jit(solution)/shard_map/all_to_all | solution.py:17
  19.9 4.6 %copy-start.1 = (bf16[2,144,2048]{2,1,0:T(8,128)(2,1)S(1)}, bf16[2,144,2048]{2,1,0:T(8,128)(2,1)}, u32[]{:S(2)}) copy-start(bf16[2,144,2048]{2,1,0:T(8,128)(2,1)} %param.7) | copy-start | bytes 3538948
  21.1 21.3 %collective-permute-start = (bf16[144,2048]{1,0:T(8,128)(2,1)}, bf16[144,2048]{1,0:T(8,128)(2,1)S(1)}, u32[]{:S(2)}, u32[]{:S(2)}) collective-permute-start(bf16[144,2048]{1,0:T(8,128)(2,1)} %get-tuple-element.11), channel_id=1, source_target_pairs={{2,0},{4,2},{6,4},{8,6},{10,8},{12,10},{14,12},{16,14},{18,16},{20... | collective-permute-start | bytes 1769480 | tf_op jit(solution)/shard_map/ppermute | solution.py:38
  25.6 23.2 %collective-permute-start.1 = (bf16[144,2048]{1,0:T(8,128)(2,1)}, bf16[144,2048]{1,0:T(8,128)(2,1)}, u32[]{:S(2)}, u32[]{:S(2)}) collective-permute-start(bf16[144,2048]{1,0:T(8,128)(2,1)} %get-tuple-element.9), channel_id=1, source_target_pairs={{2,0},{4,2},{6,4},{8,6},{10,8},{12,10},{14,12},{16,14},{18,16},{20... | collective-permute-start | bytes 1769480 | tf_op jit(solution)/shard_map/ppermute | solution.py:38
  27.6 20.2 %collective-permute-start.2 = (bf16[144,2048]{1,0:T(8,128)(2,1)}, bf16[144,2048]{1,0:T(8,128)(2,1)S(1)}, u32[]{:S(2)}, u32[]{:S(2)}) collective-permute-start(bf16[144,2048]{1,0:T(8,128)(2,1)} %get-tuple-element.10), channel_id=1, source_target_pairs={{4,0},{6,2},{8,4},{10,6},{12,8},{14,10},{16,12},{18,14},{20,16},{2... | collective-permute-start | bytes 1769480 | tf_op jit(solution)/shard_map/ppermute | solution.py:38
  30.3 30.4 %collective-permute-start.3 = (bf16[144,2048]{1,0:T(8,128)(2,1)}, bf16[144,2048]{1,0:T(8,128)(2,1)}, u32[]{:S(2)}, u32[]{:S(2)}) collective-permute-start(bf16[144,2048]{1,0:T(8,128)(2,1)} %get-tuple-element.8), channel_id=1, source_target_pairs={{4,0},{6,2},{8,4},{10,6},{12,8},{14,10},{16,12},{18,14},{20,16},{2... | collective-permute-start | bytes 1769480 | tf_op jit(solution)/shard_map/ppermute | solution.py:38
  36.5 1.0 copy-start.4
  38.8 1.3 copy-start.2
  43.1 5.8 %copy-start.8 = (bf16[2,1,128,1024]{2,3,1,0:T(8,128)(2,1)S(1)}, bf16[2,1,128,1024]{2,3,1,0:T(8,128)(2,1)}, u32[]{:S(2)}) copy-start(bf16[2,1,128,1024]{2,3,1,0:T(8,128)(2,1)} %copy-done.7) | copy-start | bytes 1572868
  68.8 30.3 %all-to-all-start.3 = ((f32[2,128,1024]{2,1,0:T(8,128)}), f32[2,128,1024]{2,1,0:T(8,128)S(1)}, u32[]{:S(2)}, u32[]{:S(2)}) async-start(f32[2,128,1024]{2,1,0:T(8,128)} %bitcast.108), calls=%async_computation.3 | async-start | bytes 2097152 | tf_op jit(solution)/shard_map/all_to_all | solution.py:48
  74.9 93.3 %collective-permute-start.4 = (f32[144,2048]{1,0:T(8,128)}, f32[144,2048]{1,0:T(8,128)}, u32[]{:S(2)}, u32[]{:S(2)}) collective-permute-start(f32[144,2048]{1,0:T(8,128)} %convolution_add_fusion.1), channel_id=1, source_target_pairs={{510,0},{0,2},{2,4},{4,6},{6,8},{8,10},{10,12},{12,14},{14,16},{16... | collective-permute-start | bytes 3538952 | tf_op jit(solution)/shard_map/ppermute | solution.py:38
  99.0 1.0 copy-start.5
  100.0 64.7 %all-to-all-start.2 = ((f32[2,1024,256]{1,2,0:T(8,128)}), f32[2,1024,256]{1,2,0:T(8,128)}, u32[]{:S(2)}, u32[]{:S(2)}) async-start(f32[2,1024,256]{1,2,0:T(8,128)} %bitcast.106), calls=%async_computation.2 | async-start | bytes 4194304 | tf_op jit(solution)/shard_map/all_to_all | solution.py:48
  104.8 1.3 copy-start.3
  108.1 9.6 %copy-start.6 = (f32[2,128,1024]{2,1,0:T(8,128)S(1)}, f32[2,128,1024]{2,1,0:T(8,128)}, u32[]{:S(2)}) copy-start(f32[2,128,1024]{2,1,0:T(8,128)} %copy-done.5) | copy-start | bytes 3145732
  108.1 62.0 %collective-permute-start.5 = (f32[144,2048]{1,0:T(8,128)}, f32[144,2048]{1,0:T(8,128)}, u32[]{:S(2)}, u32[]{:S(2)}) collective-permute-start(f32[144,2048]{1,0:T(8,128)} %convolution_add_fusion), channel_id=1, source_target_pairs={{508,0},{510,2},{0,4},{2,6},{4,8},{6,10},{8,12},{10,14},{12,16},{1... | collective-permute-start | bytes 3538952 | tf_op jit(solution)/shard_map/ppermute | solution.py:38
where the time goes:
time: 174 us; the launch traced here: 173 us
  waiting for transfers between devices  65.7 us (38%)
  starting transfers between devices  59.9 us (34%)
  local copies, waits for them, and re-layouts  16.6 us (10%)
  matrix products  16.4 us (9%)
  other arithmetic  7.3 us (4%)
  between operations  6.94 us (4%)
    all_to_all x2, waiting for transfers between devices, sent_and_summed(): parts = lax.all_to_all(in_blocks(array, dim, peers), axis, 0, 0, tiled=True)  46.2 us
    ppermute x6, starting transfers between devices, shifted(): return lax.ppermute(block, axis, route)  43.4 us
    ppermute x6, waiting for transfers between devices, shifted(): return lax.ppermute(block, axis, route)  15.2 us
    all_to_all x2, starting transfers between devices, sent_and_summed(): parts = lax.all_to_all(in_blocks(array, dim, peers), axis, 0, 0, tiled=True)  9.29 us
    all_to_all x2, starting transfers between devices, from_everyone(): lax.all_to_all(jnp.broadcast_to(array[None], (peers, *array.shape)), axis...  7.2 us
    unnamed x26, local copies, waits for them, and re-layouts  5.25 us
    dot_general x3, matrix products, slab_terms(): lax.dot_general(rows_g, w_down, by_units, preferred_element_type=jnp.floa...  4.28 us
    all_to_all x2, waiting for transfers between devices, from_everyone(): lax.all_to_all(jnp.broadcast_to(array[None], (peers, *array.shape)), axis...  4.26 us
  transfers between devices with their start and end apart: 10, of which 5 were waited for; matrix products, arithmetic and copies ran while one was open for 13% of the time, Pallas kernels for 0%

commit v1 on v0

v1 whole, which is shorter than its diff:
```python
import functools

import jax
import jax.numpy as jnp
from jax import lax
from jax.experimental import pallas as pl
from jax.experimental.pallas import tpu as pltpu
from jax.sharding import PartitionSpec as P

F32, BF16 = jnp.float32, jnp.bfloat16
BY_LAST = (((1,), (1,)), ((), ()))
BY_FIRST = (((0,), (0,)), ((), ()))
VMEM = pl.BlockSpec(memory_space=pltpu.VMEM)
SMEM = pl.BlockSpec(memory_space=pltpu.SMEM)


def step_x(b, d, by):
    x = (2 * d + (b // 2) % 2 + by) % 4
    return x % 2, x // 2


def hop(by, chips):
    def target(b, d):
        lo, hi = step_x(b, d, by)
        return (b + 2 * chips, hi)

    return target


def along_row(by):
    def target(b, d):
        lo, hi = step_x(b, d, by(b))
        return ((b // 4) * 4 + 2 * lo + b % 2, hi)

    return target


def sent(array, even, odd, mesh_sizes):
    blk, dp = mesh_sizes
    pairs = []
    for b in range(blk):
        for d in range(dp):
            rule = odd if b % 2 else even
            if rule is not None:
                tb, td = rule(b, d)
                pairs.append((b * dp + d, (tb % blk) * dp + td))
    return lax.ppermute(array, ("blk", "dp"), pairs)


def whereabouts():
    b = lax.axis_index("blk")
    return b, lax.axis_index("dp"), b % 2, (b // 2) % 2


def pack_kernel(gate_ref, up_ref, down_ref, out_ref):
    out_ref[:, :128] = gate_ref[0]
    out_ref[:, 128:256] = up_ref[0]
    out_ref[:, 256:] = down_ref[0].T


def slab_terms(x_ref, g_ref, s_ref):
    both = jnp.dot(x_ref[...], s_ref[:, :256], preferred_element_type=F32)
    hidden_grad = jnp.dot(g_ref[...], s_ref[:, 256:], preferred_element_type=F32)
    gate, up = both[:, :128], both[:, 128:]
    sig = jax.nn.sigmoid(gate)
    act = gate * sig
    hidden = (act * up).astype(BF16)
    up_in = (hidden_grad * act).astype(BF16)
    gate_in = (hidden_grad * up * sig * (1.0 + gate * (1.0 - sig))).astype(BF16)
    both_in = jnp.concatenate([gate_in, up_in], axis=1)
    return both_in, hidden


def first_kernel(
    layer_ref, x_ref, g_ref, swap_ref, own_ref, near_ref, far_ref,
    sums_ref, out_ref, dx_own_ref, dx_swap_ref,
    slab, xs, gs,
):
    b, d, core, lo = whereabouts()
    n = lax.axis_size("blk")
    rows = x_ref.shape[1]
    half = own_ref.shape[0]
    here = pl.multiple_of(d * half, half)
    there = pl.multiple_of((1 - d) * half, half)

    @pl.when(core == 0)
    def _():
        slab[pl.ds(here, half), :] = own_ref[...]
        slab[pl.ds(there, half), :] = near_ref[...]

    @pl.when(core == 1)
    def _():
        first = pl.multiple_of(((d + lo) % 2) * half, half)
        second = pl.multiple_of(((d + lo + 1) % 2) * half, half)
        slab[pl.ds(first, half), :] = near_ref[...]
        slab[pl.ds(second, half), :] = far_ref[...]

    layer = layer_ref[(b - 2 * core + n) % n]
    xs[:rows] = x_ref[layer]
    gs[:rows] = g_ref[layer]
    xs[rows:] = swap_ref[0]
    gs[rows:] = swap_ref[1]
    both_in, hidden = slab_terms(xs, gs, slab)
    dx = lax.dot_general(both_in, slab[:, :256], BY_LAST, preferred_element_type=F32)
    dx_own_ref[...] = dx[:rows]
    dx_swap_ref[...] = dx[rows:].astype(BF16)
    sums_ref[:256] = lax.dot_general(both_in, xs[...], BY_FIRST, preferred_element_type=F32)
    sums_ref[256:] = lax.dot_general(hidden, gs[...], BY_FIRST, preferred_element_type=F32)
    pick = pl.multiple_of(((d + lo) % 2) * half, half)
    out_ref[...] = sums_ref[:, pl.ds(pick, half)].astype(BF16)


def second_kernel(
    layer_ref, x_ref, g_ref, guest_ref, own_ref, near_ref, relayed_ref, sums_ref,
    mine_ref, out_ref, dx_guest_ref, dx_own_ref,
    slab, xs, gs, total,
):
    b, d, core, lo = whereabouts()
    half = own_ref.shape[0]
    here = pl.multiple_of(d * half, half)
    there = pl.multiple_of((1 - d) * half, half)
    slab[pl.ds(here, half), :] = own_ref[...]

    @pl.when(core == 0)
    def _():
        slab[pl.ds(there, half), :] = near_ref[...]
        xs[...] = guest_ref[0]
        gs[...] = guest_ref[1]

    @pl.when(core == 1)
    def _():
        slab[pl.ds(there, half), :] = relayed_ref[...]
        layer = layer_ref[b]
        xs[...] = x_ref[layer]
        gs[...] = g_ref[layer]

    both_in, hidden = slab_terms(xs, gs, slab)
    total[:256] = lax.dot_general(both_in, xs[...], BY_FIRST, preferred_element_type=F32)
    total[256:] = lax.dot_general(hidden, gs[...], BY_FIRST, preferred_element_type=F32)

    @pl.when(core == 0)
    def _():
        total[...] += sums_ref[...]

    mine_ref[...] = total[:, pl.ds(here, half)]
    out_ref[...] = total[:, pl.ds(there, half)].astype(BF16)
    dx = lax.dot_general(both_in, slab[:, :256], BY_LAST, preferred_element_type=F32)
    dx_guest_ref[...] = dx.astype(BF16)
    dx_own_ref[...] = jnp.where(core == 1, dx, 0.0)


def relay_kernel(sums_ref, got_ref, out_ref):
    b, d, core, lo = whereabouts()
    half = got_ref.shape[1]

    @pl.when(core == 0)
    def _():
        out_ref[...] = got_ref[...]

    @pl.when(core == 1)
    def _():
        pick = pl.multiple_of(((d + lo + 1) % 2) * half, half)
        out_ref[...] = (sums_ref[:, pl.ds(pick, half)] + got_ref[...].astype(F32)).astype(BF16)


def final_kernel(mine_ref, a_ref, b_ref, gate_ref, up_ref, down_ref):
    total = mine_ref[...] + a_ref[...].astype(F32) + b_ref[...].astype(F32)
    gate_ref[0] = total[:128].T.astype(BF16)
    up_ref[0] = total[128:256].T.astype(BF16)
    down_ref[0] = total[256:].astype(BF16)


def tokens_kernel(layer_ref, dx_own_ref, swap_ref, guest_ref, dx_late_ref, out_ref):
    b, d, core, lo = whereabouts()
    n = lax.axis_size("blk")
    own = layer_ref[(b - 2 * core + n) % n]
    mid = layer_ref[(b - 1 + n) % n]
    late = layer_ref[(b - 2 * (1 - core) + n) % n]
    for l in range(out_ref.shape[0]):
        out_ref[l] = (
            jnp.where(own == l, dx_own_ref[...], 0.0)
            + jnp.where(mid == l, swap_ref[...].astype(F32), 0.0)
            + jnp.where(late == l, guest_ref[...].astype(F32) + dx_late_ref[...], 0.0)
        ).astype(BF16)


def tile(shape, dtype):
    return jax.ShapeDtypeStruct(shape, dtype)


def call(body, outs, operands, scratch=(), flops=0):
    moved = sum(a.size * a.dtype.itemsize for a in operands)
    specs = [SMEM if a.dtype == jnp.int32 else VMEM for a in operands]
    return pl.pallas_call(
        body,
        out_shape=outs,
        in_specs=specs,
        out_specs=jax.tree.map(lambda _: VMEM, outs),
        scratch_shapes=list(scratch),
        cost_estimate=pl.CostEstimate(flops=flops, bytes_accessed=moved, transcendentals=0),
    )(*operands)


def on_device(acts, cotangent, w_gate, w_up, w_down, slab_layer, sizes):
    layers, rows, width = acts.shape
    half = w_gate.shape[1]
    units = w_gate.shape[2]
    send = functools.partial(sent, mesh_sizes=sizes)
    b = lax.axis_index("blk")
    n = sizes[0]

    def swap_core(b, d):
        return (b ^ 1, d)

    def swap_dp(b, d):
        return (b, 1 - d)

    own = call(pack_kernel, tile((half, 3 * units), BF16), (w_gate, w_up, w_down))
    near = send(own, swap_dp, hop(-1, 1))
    far = send(own, None, hop(1, 1))

    def rows_of(layer):
        pick = lambda a: lax.dynamic_index_in_dim(a, layer, 0, keepdims=False)
        return jnp.stack([pick(acts), pick(cotangent)])

    swap = send(rows_of(slab_layer[(b - 1) % n]), swap_core, swap_core)
    guest = send(rows_of(slab_layer[(b - 2) % n]), hop(-1, -1), None)
    relayed = send(near, None, hop(-1, -1))

    flops = 16 * rows * width * units
    sums, near_sum, dx_own, dx_swap = call(
        first_kernel,
        (
            tile((3 * units, width), F32), tile((3 * units, half), BF16),
            tile((rows, width), F32), tile((rows, width), BF16),
        ),
        (slab_layer, acts, cotangent, swap, own, near, far),
        (
            pltpu.VMEM((width, 3 * units), BF16),
            pltpu.VMEM((2 * rows, width), BF16), pltpu.VMEM((2 * rows, width), BF16),
        ),
        2 * flops,
    )
    got_near = send(near_sum, None, hop(1, -1))
    dx_swapped = send(dx_swap, swap_core, swap_core)
    mine, own_sum, dx_guest, dx_late = call(
        second_kernel,
        (
            tile((3 * units, half), F32), tile((3 * units, half), BF16),
            tile((rows, width), BF16), tile((rows, width), F32),
        ),
        (slab_layer, acts, cotangent, guest, own, near, relayed, sums),
        (
            pltpu.VMEM((width, 3 * units), BF16),
            pltpu.VMEM((rows, width), BF16), pltpu.VMEM((rows, width), BF16),
            pltpu.VMEM((3 * units, width), F32),
        ),
        flops,
    )
    passed = send(own_sum, along_row(lambda b: -1 if (b // 2) % 2 else 1), hop(-1, 1))
    dx_back = send(dx_guest, hop(1, 1), None)
    onward = call(relay_kernel, tile((3 * units, half), BF16), (sums, passed))
    got_far = send(onward, along_row(lambda b: 1 if (b // 2) % 2 else -1), hop(-1, -1))
    acts_grad = call(
        tokens_kernel, tile(acts.shape, BF16), (slab_layer, dx_own, dx_swapped, dx_back, dx_late)
    )
    grads = call(
        final_kernel,
        (tile((1, half, units), BF16), tile((1, half, units), BF16), tile((1, units, half), BF16)),
        (mine, got_near, got_far),
    )
    return (*grads, acts_grad)


def solution(mesh):
    in_specs = (
        P(None, ("blk", "dp"), None),
        P(None, ("blk", "dp"), None),
        P("blk", "dp", None),
        P("blk", "dp", None),
        P("blk", None, "dp"),
        P(),
    )
    out_specs = (
        P("blk", "dp", None),
        P("blk", "dp", None),
        P("blk", None, "dp"),
        P(None, ("blk", "dp"), None),
    )
    body = functools.partial(on_device, sizes=(mesh.shape["blk"], mesh.shape["dp"]))
    return jax.shard_map(
        body, mesh=mesh, in_specs=in_specs, out_specs=out_specs, check_vma=False
    )
```

time: 174 us -> 117 us (0.67)
  the two profiles are of different devices: /device:TPU:283 before, /device:TPU:4 now
where the time goes in v1:
time: 117 us; the launch traced here: 116 us
  waiting for transfers between devices  44.5 us (38%)
  starting transfers between devices  31.9 us (27%)
  Pallas kernels  26.9 us (23%)
  local copies, waits for them, and re-layouts  7.03 us (6%)
  between operations  4.78 us (4%)
  other arithmetic  1.23 us (1%)
    ppermute x10, waiting for transfers between devices, sent(): return lax.ppermute(array, ('blk', 'dp'), pairs)  44.5 us
    ppermute x10, starting transfers between devices, sent(): return lax.ppermute(array, ('blk', 'dp'), pairs)  31.9 us
    pallas_call x6, Pallas kernels, call(): pl.pallas_call(body, out_shape=outs, in_specs=specs, out_specs=jax.tree.m...  26.9 us
    unnamed x26, local copies, waits for them, and re-layouts  5.03 us
  transfers between devices with their start and end apart: 10, of which 3 were waited for; matrix products, arithmetic and copies ran while one was open for 3% of the time, Pallas kernels for 12%

profile of v1, /device:TPU:4, one launch (start us, length us, event | category | flops | bytes accessed | tf_op | source)
XLA Modules:
  0.0 116.4 jit_solution(692438077839349065)
XLA Ops:
  0.7 2.2 %shard_map.93.own_ref = bf16[1024,384]{1,0:T(8,128)(2,1)} custom-call(bf16[1,1024,128]{2,1,0:T(8,128)(2,1)} %gate_ref.1, bf16[1,1024,128]{2,1,0:T(8,128)(2,1)} %up_ref.1, bf16[1,128,1024]{2,1,0:T(8,128)(2,1)} %down_ref.1), custom_call_target="tpu_custom_call" | custom-call | bytes 786432 | tf_op jit(solution)/shard_map/pallas_call | solution.py:194
  2.9 7.7 %collective-permute-start.1 = (bf16[1024,384]{1,0:T(8,128)(2,1)}, bf16[1024,384]{1,0:T(8,128)(2,1)S(1)}, u32[]{:S(2)}, u32[]{:S(2)}) collective-permute-start(bf16[1024,384]{1,0:T(8,128)(2,1)} %shard_map.93.own_ref), channel_id=1, source_target_pairs={{0,1},{1,0},{2,7},{3,6},{4,5},{5,4},{6,10},{7,11},{8,9},{9,8},{10,... | collective-permute-start | bytes 2359304 | tf_op jit(solution)/shard_map/ppermute | solution.py:47
  15.2 1.4 %constant_dynamic-slice_fusion = (bf16[1,144,2048]{2,1,0:T(8,128)(2,1)S(1)}, bf16[1,144,2048]{2,1,0:T(8,128)(2,1)S(1)}, bf16[1,144,2048]{2,1,0:T(8,128)(2,1)S(1)}, bf16[1,144,2048]{2,1,0:T(8,128)(2,1)S(1)}) fusion(bf16[2,144,2048]{2,1,0:T(8,128)(2,1)} %g_ref.3, s32[]{:T(128)S(6)} %select_n.31, s32[]{:T(128)S(6)} %select_n.28, bf16[2,144,2048]{2,1,0:T(8,128)(2,1)S(1)} %copy-done), kind=kLoop, calls=%fused_computation.2 | loop fusion | bytes 4718600 | tf_op jit(solution)/shard_map/jit(dynamic_index_in_dim)/dynamic_slice | solution.py:223
  16.7 1.9 %collective-permute-start.3 = (bf16[2,144,2048]{2,1,0:T(8,128)(2,1)S(1)}, bf16[2,144,2048]{2,1,0:T(8,128)(2,1)}, u32[]{:S(2)}, u32[]{:S(2)}) collective-permute-start(bf16[2,144,2048]{2,1,0:T(8,128)(2,1)S(1)} %pad_maximum_fusion.1), channel_id=1, source_target_pairs={{0,2},{1,3},{2,0},{3,1},{4,6},{5,7},{6,4},{7,5},{8,10},{9,11},{10,... | collective-permute-start | bytes 3538952 | tf_op jit(solution)/shard_map/ppermute | solution.py:47
  18.6 1.1 pad_maximum_fusion
  19.8 10.1 %collective-permute-start = (bf16[2,144,2048]{2,1,0:T(8,128)(2,1)}, bf16[2,144,2048]{2,1,0:T(8,128)(2,1)S(1)}, u32[]{:S(2)}, u32[]{:S(2)}) collective-permute-start(bf16[2,144,2048]{2,1,0:T(8,128)(2,1)} %pad_maximum_fusion), channel_id=1, source_target_pairs={{0,509},{1,508},{4,0},{5,1},{8,5},{9,4},{12,8},{13,9},{16,13},{17,... | collective-permute-start | bytes 3538952 | tf_op jit(solution)/shard_map/ppermute | solution.py:47
  29.9 0.7 collective-permute-start.4
  32.2 7.3 %shard_map.94 = (f32[384,2048]{1,0:T(8,128)}, bf16[384,1024]{1,0:T(8,128)(2,1)}, f32[144,2048]{1,0:T(8,128)}, bf16[144,2048]{1,0:T(8,128)(2,1)}) custom-call(s32[256]{0:T(256)} %layer_ref.5, bf16[2,144,2048]{2,1,0:T(8,128)(2,1)} %x_ref.3, bf16[2,144,2048]{2,1,0:T(8,128)(2,1)} %g_ref.3, bf16[2,144,2048]{2,1,0:T(8,128)(2,1)} %collective-permute-done.3.swap_ref, ...), custom_call_target="tpu_custom_call" | custom-call | flops 1207959552 | bytes 5899264 | tf_op jit(solution)/shard_map/pallas_call | solution.py:194
  39.5 12.8 %collective-permute-done.guest_ref = bf16[2,144,2048]{2,1,0:T(8,128)(2,1)S(1)} collective-permute-done((bf16[2,144,2048]{2,1,0:T(8,128)(2,1)}, bf16[2,144,2048]{2,1,0:T(8,128)(2,1)S(1)}, u32[]{:S(2)}, u32[]{:S(2)}) %collective-permute-start) | collective-permute-done | bytes 1179680 | tf_op jit(solution)/shard_map/ppermute | solution.py:47
  52.3 1.0 copy-done.3
  53.6 7.9 %shard_map.95 = (f32[384,1024]{1,0:T(8,128)}, bf16[384,1024]{1,0:T(8,128)(2,1)}, bf16[144,2048]{1,0:T(8,128)(2,1)}, f32[144,2048]{1,0:T(8,128)}) custom-call(s32[256]{0:T(256)} %layer_ref.5, bf16[2,144,2048]{2,1,0:T(8,128)(2,1)} %x_ref.3, bf16[2,144,2048]{2,1,0:T(8,128)(2,1)} %g_ref.3, bf16[2,144,2048]{2,1,0:T(8,128)(2,1)} %copy-done.3, ...), custom_call_target="tpu_custom_call" | custom-call | flops 603979776 | bytes 9044992 | tf_op jit(solution)/shard_map/pallas_call | solution.py:194
  61.4 1.9 %collective-permute-start.6 = (bf16[384,1024]{1,0:T(8,128)(2,1)}, bf16[384,1024]{1,0:T(8,128)(2,1)S(1)}, u32[]{:S(2)}, u32[]{:S(2)}) collective-permute-start(bf16[384,1024]{1,0:T(8,128)(2,1)} %get-tuple-element.18), channel_id=1, source_target_pairs={{0,4},{1,5},{2,7},{3,6},{4,0},{5,1},{6,10},{7,11},{8,12},{9,13},{1... | collective-permute-start | bytes 2359304 | tf_op jit(solution)/shard_map/ppermute | solution.py:47
  63.4 0.7 collective-permute-start.5
  64.1 17.5 %collective-permute-done.6.got_ref = bf16[384,1024]{1,0:T(8,128)(2,1)S(1)} collective-permute-done((bf16[384,1024]{1,0:T(8,128)(2,1)}, bf16[384,1024]{1,0:T(8,128)(2,1)S(1)}, u32[]{:S(2)}, u32[]{:S(2)}) %collective-permute-start.6) | collective-permute-done | bytes 786464 | tf_op jit(solution)/shard_map/ppermute | solution.py:47
  81.6 0.9 copy-done.6
  82.5 3.0 %shard_map.96 = bf16[384,1024]{1,0:T(8,128)(2,1)} custom-call(f32[384,2048]{1,0:T(8,128)} %get-tuple-element.15.sums_ref, bf16[384,1024]{1,0:T(8,128)(2,1)} %copy-done.6), custom_call_target="tpu_custom_call" | custom-call | bytes 3932160 | tf_op jit(solution)/shard_map/pallas_call | solution.py:194
  85.5 1.9 %collective-permute-start.7 = (bf16[384,1024]{1,0:T(8,128)(2,1)}, bf16[384,1024]{1,0:T(8,128)(2,1)S(1)}, u32[]{:S(2)}, u32[]{:S(2)}) collective-permute-start(bf16[384,1024]{1,0:T(8,128)(2,1)} %shard_map.96), channel_id=1, source_target_pairs={{0,5},{1,4},{2,511},{3,510},{4,1},{5,0},{6,2},{7,3},{8,13},{9,12},... | collective-permute-start | bytes 2359304 | tf_op jit(solution)/shard_map/ppermute | solution.py:47
  87.4 1.9 %collective-permute-start.8 = (bf16[144,2048]{1,0:T(8,128)(2,1)}, bf16[144,2048]{1,0:T(8,128)(2,1)S(1)}, u32[]{:S(2)}, u32[]{:S(2)}) collective-permute-start(bf16[144,2048]{1,0:T(8,128)(2,1)} %get-tuple-element.23), channel_id=1, source_target_pairs={{0,2},{1,3},{2,0},{3,1},{4,6},{5,7},{6,4},{7,5},{8,10},{9,11},{10,... | collective-permute-start | bytes 1769480 | tf_op jit(solution)/shard_map/ppermute | solution.py:47
  89.3 4.3 %collective-permute-start.9 = (bf16[144,2048]{1,0:T(8,128)(2,1)}, bf16[144,2048]{1,0:T(8,128)(2,1)S(1)}, u32[]{:S(2)}, u32[]{:S(2)}) collective-permute-start(bf16[144,2048]{1,0:T(8,128)(2,1)} %get-tuple-element.24), channel_id=1, source_target_pairs={{0,4},{1,5},{4,9},{5,8},{8,12},{9,13},{12,17},{13,16},{16,20},{17,... | collective-permute-start | bytes 1769480 | tf_op jit(solution)/shard_map/ppermute | solution.py:47
  93.6 14.2 %collective-permute-done.9.guest_ref = bf16[144,2048]{1,0:T(8,128)(2,1)S(1)} collective-permute-done((bf16[144,2048]{1,0:T(8,128)(2,1)}, bf16[144,2048]{1,0:T(8,128)(2,1)S(1)}, u32[]{:S(2)}, u32[]{:S(2)}) %collective-permute-start.9) | collective-permute-done | bytes 589856 | tf_op jit(solution)/shard_map/ppermute | solution.py:47
  107.9 0.8 copy-done.10
  108.7 3.6 %shard_map.98 = bf16[2,144,2048]{2,1,0:T(8,128)(2,1)} custom-call(s32[256]{0:T(256)} %layer_ref.5, f32[144,2048]{1,0:T(8,128)} %get-tuple-element.22.dx_own_ref, bf16[144,2048]{1,0:T(8,128)(2,1)} %copy-done.9, bf16[144,2048]{1,0:T(8,128)(2,1)} %copy-done.10, f32[144,2048]{1,0:T(8,128)} %get-tuple-element.25.dx_late_ref), custom_call_target="tpu_custom_call" | custom-call | bytes 3539968 | tf_op jit(solution)/shard_map/pallas_call | solution.py:194
  112.3 0.9 copy-done.7
  113.5 2.9 %shard_map.97 = (bf16[1,1024,128]{2,1,0:T(8,128)(2,1)}, bf16[1,1024,128]{2,1,0:T(8,128)(2,1)}, bf16[1,128,1024]{2,1,0:T(8,128)(2,1)}) custom-call(f32[384,1024]{1,0:T(8,128)} %get-tuple-element.16.mine_ref, bf16[384,1024]{1,0:T(8,128)(2,1)} %copy-done.7, bf16[384,1024]{1,0:T(8,128)(2,1)} %copy-done.8), custom_call_target="tpu_custom_call" | custom-call | bytes 3145728 | tf_op jit(solution)/shard_map/pallas_call | solution.py:194
  (32 shorter events, 2.9 us)
Async XLA Ops:
  0.6 10.1 %copy-start.11 = (s32[256]{0:T(256)S(1)}, s32[256]{0:T(256)}, u32[]{:S(2)}) copy-start(s32[256]{0:T(256)} %layer_ref.5) | copy-start | bytes 3076
  0.6 14.5 %copy-start = (bf16[2,144,2048]{2,1,0:T(8,128)(2,1)S(1)}, bf16[2,144,2048]{2,1,0:T(8,128)(2,1)}, u32[]{:S(2)}) copy-start(bf16[2,144,2048]{2,1,0:T(8,128)(2,1)} %x_ref.3) | copy-start | bytes 3538948
  2.9 27.7 %collective-permute-start.1 = (bf16[1024,384]{1,0:T(8,128)(2,1)}, bf16[1024,384]{1,0:T(8,128)(2,1)S(1)}, u32[]{:S(2)}, u32[]{:S(2)}) collective-permute-start(bf16[1024,384]{1,0:T(8,128)(2,1)} %shard_map.93.own_ref), channel_id=1, source_target_pairs={{0,1},{1,0},{2,7},{3,6},{4,5},{5,4},{6,10},{7,11},{8,9},{9,8},{10,... | collective-permute-start | bytes 2359304 | tf_op jit(solution)/shard_map/ppermute | solution.py:47
  16.7 14.6 %collective-permute-start.3 = (bf16[2,144,2048]{2,1,0:T(8,128)(2,1)S(1)}, bf16[2,144,2048]{2,1,0:T(8,128)(2,1)}, u32[]{:S(2)}, u32[]{:S(2)}) collective-permute-start(bf16[2,144,2048]{2,1,0:T(8,128)(2,1)S(1)} %pad_maximum_fusion.1), channel_id=1, source_target_pairs={{0,2},{1,3},{2,0},{3,1},{4,6},{5,7},{6,4},{7,5},{8,10},{9,11},{10,... | collective-permute-start | bytes 3538952 | tf_op jit(solution)/shard_map/ppermute | solution.py:47
  18.6 11.2 %copy-start.1 = (bf16[1024,384]{1,0:T(8,128)(2,1)S(1)}, bf16[1024,384]{1,0:T(8,128)(2,1)}, u32[]{:S(2)}) copy-start(bf16[1024,384]{1,0:T(8,128)(2,1)} %shard_map.93.own_ref) | copy-start | bytes 2359300
  19.8 32.5 %collective-permute-start = (bf16[2,144,2048]{2,1,0:T(8,128)(2,1)}, bf16[2,144,2048]{2,1,0:T(8,128)(2,1)S(1)}, u32[]{:S(2)}, u32[]{:S(2)}) collective-permute-start(bf16[2,144,2048]{2,1,0:T(8,128)(2,1)} %pad_maximum_fusion), channel_id=1, source_target_pairs={{0,509},{1,508},{4,0},{5,1},{8,5},{9,4},{12,8},{13,9},{16,13},{17,... | collective-permute-start | bytes 3538952 | tf_op jit(solution)/shard_map/ppermute | solution.py:47
  29.9 1.5 %collective-permute-start.4 = (bf16[1024,384]{1,0:T(8,128)(2,1)S(1)}, bf16[1024,384]{1,0:T(8,128)(2,1)S(1)}, u32[]{:S(2)}, u32[]{:S(2)}) collective-permute-start(bf16[1024,384]{1,0:T(8,128)(2,1)S(1)} %copy-done.1), channel_id=1, source_target_pairs={{2,6},{3,7},{6,11},{7,10},{10,14},{11,15},{14,19},{15,18},{18,22},... | collective-permute-start | bytes 2359304 | tf_op jit(solution)/shard_map/ppermute | solution.py:47
  30.6 0.9 copy-start.2
  30.6 21.7 %collective-permute-start.2 = (bf16[1024,384]{1,0:T(8,128)(2,1)S(1)}, bf16[1024,384]{1,0:T(8,128)(2,1)S(1)}, u32[]{:S(2)}, u32[]{:S(2)}) collective-permute-start(bf16[1024,384]{1,0:T(8,128)(2,1)S(1)} %collective-permute-done.1.near_ref), channel_id=1, source_target_pairs={{2,511},{3,510},{6,2},{7,3},{10,7},{11,6},{14,10},{15,11},{18,15},... | collective-permute-start | bytes 2359304 | tf_op jit(solution)/shard_map/ppermute | solution.py:47
  31.3 0.9 copy-start.5
  52.3 1.0 copy-start.3
  52.3 1.3 %copy-start.4 = (bf16[1024,384]{1,0:T(8,128)(2,1)}, bf16[1024,384]{1,0:T(8,128)(2,1)S(1)}, u32[]{:S(2)}) copy-start(bf16[1024,384]{1,0:T(8,128)(2,1)S(1)} %collective-permute-done.2.relayed_ref) | copy-start | bytes 2359300
  53.6 9.8 %copy-start.12 = (bf16[384,1024]{1,0:T(8,128)(2,1)S(1)}, bf16[384,1024]{1,0:T(8,128)(2,1)}, u32[]{:S(2)}) copy-start(bf16[384,1024]{1,0:T(8,128)(2,1)} %get-tuple-element.17) | copy-start | bytes 2359300
  61.4 20.1 %collective-permute-start.6 = (bf16[384,1024]{1,0:T(8,128)(2,1)}, bf16[384,1024]{1,0:T(8,128)(2,1)S(1)}, u32[]{:S(2)}, u32[]{:S(2)}) collective-permute-start(bf16[384,1024]{1,0:T(8,128)(2,1)} %get-tuple-element.18), channel_id=1, source_target_pairs={{0,4},{1,5},{2,7},{3,6},{4,0},{5,1},{6,10},{7,11},{8,12},{9,13},{1... | collective-permute-start | bytes 2359304 | tf_op jit(solution)/shard_map/ppermute | solution.py:47
  63.4 48.9 %collective-permute-start.5 = (bf16[384,1024]{1,0:T(8,128)(2,1)S(1)}, bf16[384,1024]{1,0:T(8,128)(2,1)S(1)}, u32[]{:S(2)}, u32[]{:S(2)}) collective-permute-start(bf16[384,1024]{1,0:T(8,128)(2,1)S(1)} %copy-done.12), channel_id=1, source_target_pairs={{2,510},{3,511},{6,3},{7,2},{10,6},{11,7},{14,11},{15,10},{18,14},... | collective-permute-start | bytes 2359304 | tf_op jit(solution)/shard_map/ppermute | solution.py:47
  81.6 0.9 copy-start.6
  85.5 26.8 %collective-permute-start.7 = (bf16[384,1024]{1,0:T(8,128)(2,1)}, bf16[384,1024]{1,0:T(8,128)(2,1)S(1)}, u32[]{:S(2)}, u32[]{:S(2)}) collective-permute-start(bf16[384,1024]{1,0:T(8,128)(2,1)} %shard_map.96), channel_id=1, source_target_pairs={{0,5},{1,4},{2,511},{3,510},{4,1},{5,0},{6,2},{7,3},{8,13},{9,12},... | collective-permute-start | bytes 2359304 | tf_op jit(solution)/shard_map/ppermute | solution.py:47
  87.4 6.2 %collective-permute-start.8 = (bf16[144,2048]{1,0:T(8,128)(2,1)}, bf16[144,2048]{1,0:T(8,128)(2,1)S(1)}, u32[]{:S(2)}, u32[]{:S(2)}) collective-permute-start(bf16[144,2048]{1,0:T(8,128)(2,1)} %get-tuple-element.23), channel_id=1, source_target_pairs={{0,2},{1,3},{2,0},{3,1},{4,6},{5,7},{6,4},{7,5},{8,10},{9,11},{10,... | collective-permute-start | bytes 1769480 | tf_op jit(solution)/shard_map/ppermute | solution.py:47
  89.3 18.6 %collective-permute-start.9 = (bf16[144,2048]{1,0:T(8,128)(2,1)}, bf16[144,2048]{1,0:T(8,128)(2,1)S(1)}, u32[]{:S(2)}, u32[]{:S(2)}) collective-permute-start(bf16[144,2048]{1,0:T(8,128)(2,1)} %get-tuple-element.24), channel_id=1, source_target_pairs={{0,4},{1,5},{4,9},{5,8},{8,12},{9,13},{12,17},{13,16},{16,20},{17,... | collective-permute-start | bytes 1769480 | tf_op jit(solution)/shard_map/ppermute | solution.py:47
  93.6 14.3 %copy-start.9 = (bf16[144,2048]{1,0:T(8,128)(2,1)}, bf16[144,2048]{1,0:T(8,128)(2,1)S(1)}, u32[]{:S(2)}) copy-start(bf16[144,2048]{1,0:T(8,128)(2,1)S(1)} %collective-permute-done.8.swap_ref) | copy-start | bytes 1769476
  107.9 0.8 copy-start.10
  112.3 0.9 copy-start.7
  112.3 1.2 %copy-start.8 = (bf16[384,1024]{1,0:T(8,128)(2,1)}, bf16[384,1024]{1,0:T(8,128)(2,1)S(1)}, u32[]{:S(2)}) copy-start(bf16[384,1024]{1,0:T(8,128)(2,1)S(1)} %collective-permute-done.7.b_ref) | copy-start | bytes 2359300
